TPU v7x, 512 devices: a whole 4x8x8 slice. The times are simulated.
512 devices in a mesh: ep: 128 (over y, z, core), rep: 4 (over x).
Axes of the slice: x: 4, y: 8, z: 8, core: 2. Of those that a mesh axis runs over, the one named last changes fastest.
Arguments:
- tokens: bfloat16 [2048, 3584], P('ep', 'rep'), may hold values from -6 to 6
- expert_ids: int32 [2048, 8], P('ep'), may hold values from 0 to 127, all different within a row; in each aligned block of 16 rows (0 to 15, 16 to 31, ...) at most 2 rows name the same one
- gate_weights: float32 [2048, 8], P('ep'), may hold values from 0.05 to 0.5
- up_weight: bfloat16 [128, 3584, 1024], P('ep', 'rep'), may hold values from -0.09375 to 0.09375
- down_weight: bfloat16 [128, 1024, 3584], P('ep', None, 'rep'), may hold values from -0.1875 to 0.1875
Outputs:
- mixture: bfloat16 [2048, 3584], P('ep', 'rep')
Inputs may be any that keep to these rules, and one draw needn't show every extreme that they name: `expert_ids`: the 8 experts of a token differ. Within the rows of one device (each aligned block of 16 tokens) no expert is named by more than 2 tokens, a bound that some block reaches.
All inputs are finite; a program needn't handle non-finite values.
Results may differ from a plain program's by a relative error of at most 0.017.
Values may be sent and summed in bfloat16 or wider, within the bound.
A program may use at most 64 MiB of HBM per device.

v0:
```python
import jax
import jax.numpy as jnp
from jax import lax
from jax.sharding import PartitionSpec as P


def local(tokens, expert_ids, gate_weights, up_weight, down_weight):
    n_peers = lax.axis_size("ep")
    tok_rows, top_count = expert_ids.shape
    width_part = tokens.shape[1]
    capacity = min(tok_rows, max(2, 3 * tok_rows * top_count // (2 * n_peers)))
    flat_ids = expert_ids.reshape(-1)
    onehot = (flat_ids[:, None] == jnp.arange(n_peers, dtype=jnp.int32)[None, :]).astype(jnp.int32)
    before = jnp.cumsum(onehot, axis=0) - onehot
    ranking = jnp.sum(before * onehot, axis=1)
    slot_index = flat_ids * capacity + ranking
    token_of_row = jnp.arange(tok_rows * top_count, dtype=jnp.int32) // top_count
    outbound = (
        jnp.zeros((n_peers * capacity, width_part), tokens.dtype)
        .at[slot_index]
        .set(tokens[token_of_row])
    )
    inbound = lax.all_to_all(outbound, "ep", split_axis=0, concat_axis=0, tiled=True)
    up_local = up_weight[0]
    down_local = down_weight[0]
    partial_pre = jnp.dot(inbound, up_local, preferred_element_type=jnp.float32)
    pre_total = lax.psum(partial_pre.astype(jnp.bfloat16), "rep").astype(jnp.float32)
    hidden = jax.nn.silu(pre_total).astype(jnp.bfloat16)
    expert_out = jnp.dot(hidden, down_local, preferred_element_type=jnp.float32).astype(
        jnp.bfloat16
    )
    returned = lax.all_to_all(expert_out, "ep", split_axis=0, concat_axis=0, tiled=True)
    picked = returned[slot_index].astype(jnp.float32).reshape(tok_rows, top_count, width_part)
    mixture = jnp.sum(gate_weights[:, :, None] * picked, axis=1)
    return mixture.astype(jnp.bfloat16)


def solution(mesh):
    placed = (
        P("ep", "rep"),
        P("ep", None),
        P("ep", None),
        P("ep", "rep", None),
        P("ep", None, "rep"),
    )
    return jax.shard_map(
        local, mesh=mesh, in_specs=placed, out_specs=P("ep", "rep"), check_vma=False
    )
```

profile of v0, /device:TPU:1, one launch (start us, length us, event | category | flops | bytes accessed | tf_op | source)
XLA Modules:
  0.0 142.5 jit_solution(13055652494298791884)
XLA Ops:
  6.5 0.0 copy-start
  6.5 0.0 all-reduce.2.cloned.1.call-start
  6.5 0.9 copy.11
  7.4 0.7 broadcast_multiply_fusion
  8.1 0.1 eq.15
  8.2 0.1 fusion.20
  8.3 0.2 reduce_window_sum.11
  8.5 0.2 select_reduce_fusion
  8.7 0.1 copy.10
  8.7 0.1 mul.34
  8.9 3.2 %scatter_custom_fusion = bf16[256,896]{1,0:T(8,128)(2,1)S(1)} fusion(s32[128]{0:T(128)S(1)} %fusion.22, bf16[16,896]{1,0:T(8,128)(2,1)} %param.5, s32[1024]{0:T(1024)S(1)} %pad_clamp_fusion.1, bf16[]{:T(256)} %constant.26.clone.1), kind=kCustom, calls=%fused_computation.18 | custom fusion | bytes 459264 | tf_op jit(solution)/shard_map/scatter | solution.py:21
  12.1 0.2 all_to_all.16
  12.3 36.4 %all_to_all.24 = bf16[128,2,896]{2,1,0:T(2,128)(2,1)S(1)} all-to-all(bf16[128,2,896]{2,1,0:T(2,128)(2,1)S(1)} %all_to_all.16), channel_id=1, replica_groups=mesh['ep'=128,'rep'=4] {'ep'}, dimensions={0} | all-to-all | bytes 917504 | tf_op jit(solution)/shard_map/all_to_all | solution.py:23
  48.7 0.2 all_to_all.18
  48.9 0.0 copy-done
  48.9 1.6 %fusion.4 = bf16[256,1024]{1,0:T(8,128)(2,1)} fusion(bf16[256,896]{1,0:T(8,128)(2,1)S(1)} %all_to_all.18, bf16[1,896,1024]{2,1,0:T(8,128)(2,1)S(1)} %copy-done), kind=kOutput, calls=%fused_computation.9 | convolution fusion | flops 470024192 | bytes 2818048 | tf_op jit(solution)/shard_map/dot_general | solution.py:26
  50.5 0.0 all-reduce.2.cloned.1.call-update
  50.5 45.2 %all-reduce.2.cloned.1.call-done = bf16[256,1024]{1,0:T(8,128)(2,1)} async-done(((bf16[256,1024]{1,0:T(8,128)(2,1)}), bf16[256,1024]{1,0:T(8,128)(2,1)}) %all-reduce.2.cloned.1.call-update) | async-done | bytes 524304 | tf_op jit(solution)/shard_map/psum | solution.py:27
  95.7 2.4 %fusion.7 = bf16[256,896]{1,0:T(8,128)(2,1)S(1)} fusion(bf16[1,1024,896]{2,1,0:T(8,128)(2,1)} %param.9, bf16[256,1024]{1,0:T(8,128)(2,1)} %all-reduce.2.cloned.1.call-done), kind=kOutput, calls=%fused_computation.10 | convolution fusion | flops 471564288 | bytes 2818048 | tf_op jit(solution)/shard_map/dot_general | solution.py:29
  98.1 0.0 copy-start.1
  98.1 0.9 all_to_all.19
  99.0 16.5 %all-to-all-start.1 = ((bf16[128,2,896]{2,1,0:T(2,128)(2,1)}), bf16[128,2,896]{2,1,0:T(2,128)(2,1)S(1)}, u32[]{:S(2)}, u32[]{:S(2)}) async-start(bf16[128,2,896]{2,1,0:T(2,128)(2,1)} %all_to_all.19), calls=%async_computation.1 | async-start | bytes 917504 | tf_op jit(solution)/shard_map/all_to_all | solution.py:32
  115.5 0.0 copy-done.1
  115.5 0.1 copy.9
  115.6 18.1 %all-to-all-done.1 = bf16[128,2,896]{2,1,0:T(2,128)(2,1)S(1)} async-done(((bf16[128,2,896]{2,1,0:T(2,128)(2,1)}), bf16[128,2,896]{2,1,0:T(2,128)(2,1)S(1)}, u32[]{:S(2)}, u32[]{:S(2)}) %all-to-all-start.1) | async-done | bytes 458784 | tf_op jit(solution)/shard_map/all_to_all | solution.py:32
  133.7 0.2 all_to_all.21
  133.9 0.9 gather_fusion
  134.8 0.8 fusion.16
  (4 shorter events, 0.0 us)
Async XLA Ops:
  6.5 42.3 %copy-start = (bf16[1,896,1024]{2,1,0:T(8,128)(2,1)S(1)}, bf16[1,896,1024]{2,1,0:T(8,128)(2,1)}, u32[]{:S(2)}) copy-start(bf16[1,896,1024]{2,1,0:T(8,128)(2,1)} %param.8) | copy-start | bytes 5505028
  6.5 89.1 %all-reduce.2.cloned.1.call-start = ((), (), s32[]{:S(2)}) async-start(), calls=%async_computation.2 | async-start | bytes 1048576 | tf_op jit(solution)/shard_map/psum | solution.py:27
  98.1 17.4 %copy-start.1 = (f32[16,8]{0,1:T(8,128)S(1)}, f32[16,8]{0,1:T(8,128)}, u32[]{:S(2)}) copy-start(f32[16,8]{0,1:T(8,128)} %param.7) | copy-start | bytes 1540
  99.0 34.7 %all-to-all-start.1 = ((bf16[128,2,896]{2,1,0:T(2,128)(2,1)}), bf16[128,2,896]{2,1,0:T(2,128)(2,1)S(1)}, u32[]{:S(2)}, u32[]{:S(2)}) async-start(bf16[128,2,896]{2,1,0:T(2,128)(2,1)} %all_to_all.19), calls=%async_computation.1 | async-start | bytes 917504 | tf_op jit(solution)/shard_map/all_to_all | solution.py:32
Sparse Core Ops, SparseCore 0:
  50.6 45.0 all-reduce.1
where the time goes:
time: 143 us; the launch traced here: 142 us
  waiting for transfers between devices  63.3 us (44%)
  blocking collectives  36.4 us (25%)
  starting transfers between devices  16.5 us (12%)
  between operations  13.5 us (9%)
  local copies, waits for them, and re-layouts  6.8 us (5%)
  matrix products  3.98 us (3%)
  other arithmetic  1.96 us (1%)
    psum x1, waiting for transfers between devices, local(): lax.psum(partial_pre.astype(jnp.bfloat16), 'rep').astype(jnp.float32)  45.2 us
    all_to_all x1, blocking collectives, local(): lax.all_to_all(outbound, 'ep', split_axis=0, concat_axis=0, tiled=True)  36.4 us
    all_to_all x1, waiting for transfers between devices, local(): lax.all_to_all(expert_out, 'ep', split_axis=0, concat_axis=0, tiled=True)  18.1 us
    all_to_all x1, starting transfers between devices, local(): lax.all_to_all(expert_out, 'ep', split_axis=0, concat_axis=0, tiled=True)  16.5 us
    scatter x1, local copies, waits for them, and re-layouts, local(): outbound = jnp.zeros((n_peers * capacity, width_part), tokens.dtype).at[s...  3.23 us
  transfers between devices with their start and end apart: 2, of which 2 were waited for; matrix products, arithmetic and copies ran while one was open for 0% of the time, Pallas kernels for 0%

commit v1 on v0

--- a/solution.py
+++ b/solution.py
@@ -24,7 +24,9 @@
     up_local = up_weight[0]
     down_local = down_weight[0]
     partial_pre = jnp.dot(inbound, up_local, preferred_element_type=jnp.float32)
-    pre_total = lax.psum(partial_pre.astype(jnp.bfloat16), "rep").astype(jnp.float32)
+    pre_total = jnp.sum(lax.all_gather(partial_pre.astype(jnp.bfloat16), "rep"), 0).astype(
+        jnp.float32
+    )
     hidden = jax.nn.silu(pre_total).astype(jnp.bfloat16)
     expert_out = jnp.dot(hidden, down_local, preferred_element_type=jnp.float32).astype(
         jnp.bfloat16

time: 143 us -> 127 us (0.89)
  waiting for transfers between devices: 63.3 us -> 47.6 us
  starting transfers between devices: 16.5 us -> 14.4 us
  other arithmetic: 1.96 us -> 3.99 us
    psum x1 -> x0, waiting for transfers between devices: 45.2 us -> none  [local(): lax.psum(partial_pre.astype(jnp.bfloat16), 'rep').astype(jnp.float32)]
    all_gather x0 -> x1, waiting for transfers between devices: none -> 29.5 us  [local(): lax.all_gather(partial_pre.astype(jnp.bfloat16), 'rep')]
    all_to_all x1, starting transfers between devices: 16.5 us -> 14.4 us  [local(): lax.all_to_all(expert_out, 'ep', split_axis=0, concat_axis=0, tiled=True)]
    reduce_sum x0 -> x1, other arithmetic: none -> 2.02 us  [local(): jnp.sum(lax.all_gather(partial_pre.astype(jnp.bfloat16), 'rep'), 0)]
where the time goes in v1:
time: 127 us
  waiting for transfers between devices  47.6 us (37%)
  blocking collectives  36.4 us (29%)
  starting transfers between devices  14.4 us (11%)
  between operations  13.5 us (11%)
  local copies, waits for them, and re-layouts  7.08 us (6%)
  other arithmetic  3.99 us (3%)
  matrix products  3.84 us (3%)
    all_to_all x1, blocking collectives, local(): lax.all_to_all(outbound, 'ep', split_axis=0, concat_axis=0, tiled=True)  36.4 us
    all_gather x1, waiting for transfers between devices, local(): lax.all_gather(partial_pre.astype(jnp.bfloat16), 'rep')  29.5 us
    all_to_all x1, waiting for transfers between devices, local(): lax.all_to_all(expert_out, 'ep', split_axis=0, concat_axis=0, tiled=True)  18.1 us
    all_to_all x1, starting transfers between devices, local(): lax.all_to_all(expert_out, 'ep', split_axis=0, concat_axis=0, tiled=True)  14.4 us
    scatter x1, local copies, waits for them, and re-layouts, local(): outbound = jnp.zeros((n_peers * capacity, width_part), tokens.dtype).at[s...  3.51 us
  transfers between devices with their start and end apart: 2, of which 2 were waited for; matrix products, arithmetic and copies ran while one was open for 0% of the time, Pallas kernels for 0%

profile of v1, /device:TPU:1, one launch (start us, length us, event | category | flops | bytes accessed | tf_op | source)
XLA Modules:
  0.0 126.9 jit_solution(14805645848831851307)
XLA Ops:
  6.5 0.0 copy-start
  6.5 0.0 all-gather.3.cloned.1.call-start
  6.5 0.9 copy.11
  7.4 0.7 broadcast_multiply_fusion
  8.1 0.1 eq.15
  8.2 0.1 fusion.20
  8.3 0.2 reduce_window_sum.11
  8.5 0.2 select_reduce_fusion
  8.7 0.1 copy.10
  8.7 0.1 mul.34
  8.9 3.5 %scatter_custom_fusion = bf16[256,896]{1,0:T(8,128)(2,1)S(1)} fusion(s32[128]{0:T(128)S(1)} %fusion.22, bf16[16,896]{1,0:T(8,128)(2,1)} %param.5, s32[1024]{0:T(1024)S(1)} %pad_clamp_fusion.1, bf16[]{:T(256)} %constant.27.clone.1), kind=kCustom, calls=%fused_computation.18 | custom fusion | bytes 459264 | tf_op jit(solution)/shard_map/scatter | solution.py:21
  12.4 0.2 all_to_all.16
  12.6 36.4 %all_to_all.24 = bf16[128,2,896]{2,1,0:T(2,128)(2,1)S(1)} all-to-all(bf16[128,2,896]{2,1,0:T(2,128)(2,1)S(1)} %all_to_all.16), channel_id=1, replica_groups=mesh['ep'=128,'rep'=4] {'ep'}, dimensions={0} | all-to-all | bytes 917504 | tf_op jit(solution)/shard_map/all_to_all | solution.py:23
  49.0 0.2 all_to_all.18
  49.2 0.0 copy-done
  49.2 1.5 %fusion.4 = bf16[256,1024]{1,0:T(8,128)(2,1)} fusion(bf16[256,896]{1,0:T(8,128)(2,1)S(1)} %all_to_all.18, bf16[1,896,1024]{2,1,0:T(8,128)(2,1)S(1)} %copy-done), kind=kOutput, calls=%fused_computation.9 | convolution fusion | flops 470024192 | bytes 2818048 | tf_op jit(solution)/shard_map/dot_general | solution.py:26
  50.7 0.0 all-gather.3.cloned.1.call-update
  50.7 29.5 %all-gather.3.cloned.1.call-done = bf16[1024,1024]{1,0:T(8,128)(2,1)} async-done(((bf16[256,1024]{1,0:T(8,128)(2,1)}), bf16[1024,1024]{1,0:T(8,128)(2,1)}) %all-gather.3.cloned.1.call-update) | async-done | bytes 2097168 | tf_op jit(solution)/shard_map/all_gather | solution.py:27
  80.2 2.0 %reduce_sum.34 = bf16[256,1024]{1,0:T(8,128)(2,1)S(1)} reduce(bf16[4,256,1024]{2,1,0:T(8,128)(2,1)} %bitcast.23, bf16[]{:T(256)} %constant.27.clone.1), dimensions={0}, to_apply=%region_3.4 | reduce | flops 786432 | bytes 2621442 | tf_op jit(solution)/shard_map/reduce_sum | solution.py:27
  82.3 2.3 %fusion.7 = bf16[256,896]{1,0:T(8,128)(2,1)S(1)} fusion(bf16[1,1024,896]{2,1,0:T(8,128)(2,1)} %param.9, bf16[256,1024]{1,0:T(8,128)(2,1)S(1)} %reduce_sum.34), kind=kOutput, calls=%fused_computation.10 | convolution fusion | flops 471564288 | bytes 2818048 | tf_op jit(solution)/shard_map/dot_general | solution.py:31
  84.6 0.0 copy-start.1
  84.6 0.9 all_to_all.19
  85.5 14.4 %all-to-all-start.1 = ((bf16[128,2,896]{2,1,0:T(2,128)(2,1)}), bf16[128,2,896]{2,1,0:T(2,128)(2,1)S(1)}, u32[]{:S(2)}, u32[]{:S(2)}) async-start(bf16[128,2,896]{2,1,0:T(2,128)(2,1)} %all_to_all.19), calls=%async_computation.1 | async-start | bytes 917504 | tf_op jit(solution)/shard_map/all_to_all | solution.py:34
  100.0 0.0 copy-done.1
  100.0 0.1 copy.9
  100.0 18.1 %all-to-all-done.1 = bf16[128,2,896]{2,1,0:T(2,128)(2,1)S(1)} async-done(((bf16[128,2,896]{2,1,0:T(2,128)(2,1)}), bf16[128,2,896]{2,1,0:T(2,128)(2,1)S(1)}, u32[]{:S(2)}, u32[]{:S(2)}) %all-to-all-start.1) | async-done | bytes 458784 | tf_op jit(solution)/shard_map/all_to_all | solution.py:34
  118.2 0.2 all_to_all.21
  118.4 0.9 gather_fusion
  119.2 0.8 fusion.16
  (4 shorter events, 0.0 us)
Async XLA Ops:
  6.5 42.6 %copy-start = (bf16[1,896,1024]{2,1,0:T(8,128)(2,1)S(1)}, bf16[1,896,1024]{2,1,0:T(8,128)(2,1)}, u32[]{:S(2)}) copy-start(bf16[1,896,1024]{2,1,0:T(8,128)(2,1)} %param.8) | copy-start | bytes 5505028
  6.5 73.7 %all-gather.3.cloned.1.call-start = ((), (), s32[]{:S(2)}) async-start(), calls=%async_computation.2 | async-start | bytes 2621440 | tf_op jit(solution)/shard_map/all_gather | solution.py:27
  84.6 15.4 %copy-start.1 = (f32[16,8]{0,1:T(8,128)S(1)}, f32[16,8]{0,1:T(8,128)}, u32[]{:S(2)}) copy-start(f32[16,8]{0,1:T(8,128)} %param.7) | copy-start | bytes 1540
  85.5 32.7 %all-to-all-start.1 = ((bf16[128,2,896]{2,1,0:T(2,128)(2,1)}), bf16[128,2,896]{2,1,0:T(2,128)(2,1)S(1)}, u32[]{:S(2)}, u32[]{:S(2)}) async-start(bf16[128,2,896]{2,1,0:T(2,128)(2,1)} %all_to_all.19), calls=%async_computation.1 | async-start | bytes 917504 | tf_op jit(solution)/shard_map/all_to_all | solution.py:34
Sparse Core Ops, SparseCore 0:
  50.9 29.3 all-gather.2
